TPU v7x, 32 devices: a whole 2x2x4 slice. The times are simulated.
32 devices in a mesh: rows: 4 (over y, core), cols: 8 (over z, x).
Axes of the slice: x: 2, y: 2, z: 4, core: 2. Of those that a mesh axis runs over, the one named last changes fastest.
Arguments:
- costs: bfloat16 [4, 8, 24, 256, 256], P('rows', 'cols'), may hold values from -210 to 8
- block_rows: int32 [4, 8, 24], P('rows', 'cols'), may hold values from 0 to 7, as said below
- block_cols: int32 [4, 8, 24], P('rows', 'cols'), may hold values from 0 to 63, as said below
- live: int32 [4, 8], P('rows', 'cols'), may hold values from 16 to 24, as said below
- log_source: float32 [8192], P('rows'), may hold values from -6 to 6
- log_target: float32 [131072], P('cols'), may hold values from -6 to 6
Outputs:
- source_potential: float32 [8192], P('rows')
- target_potential: float32 [131072], P('cols')
Inputs may be any that keep to these rules, and one draw needn't show every extreme that they name: `block_rows`: row blocks are local to a device's 8 blocks of source cells. `block_cols`: column blocks are local to a device's 64 blocks of target cells. Every source cell and every target cell lies in some live block. `live`: live counts differ from device to device; some device uses all 24 slots.
All inputs are finite; a program needn't handle non-finite values.
Results may differ from a plain program's by a relative error of at most 0.0003.
Values sent between devices are 32-bit elements; how exact they have to be, the bound alone decides.
A program may use at most 64 MiB of HBM per device.

v0:
```python
import jax
import jax.numpy as jnp
from jax import lax
from jax.sharding import PartitionSpec as P

ITERS = 3


NEG = -1e30


def combined_all(value, axis, combine):
    everything = jax.tree.map(lambda part: lax.all_gather(part, axis), value)
    first = jax.tree.map(lambda part: part[0], everything)

    def hop(k, so_far):
        return combine(so_far, jax.tree.map(lambda part: part[k], everything))

    return lax.fori_loop(1, lax.axis_size(axis), hop, first)


def combine(first, second):
    top_a, tot_a = first
    top_b, tot_b = second
    top = jnp.maximum(top_a, top_b)
    return (top, tot_a * jnp.exp(top_a - top) + tot_b * jnp.exp(top_b - top))


def block_reduce(slot_top, score_fn, blocks_of, blocks, valid):
    select = (blocks_of[:, None] == jnp.arange(blocks, dtype=jnp.int32)[None, :]) & valid[:, None]
    block_top = jnp.max(jnp.where(select[:, :, None], slot_top[:, None, :], NEG), axis=0)
    own_top = jnp.max(jnp.where(select[:, :, None], block_top[None, :, :], NEG), axis=1)
    own_top = jnp.where(valid[:, None], own_top, 0.0)
    sums = score_fn(own_top)
    sums = jnp.where(valid[:, None], sums, 0.0)
    total = jnp.sum(jnp.where(select[:, :, None], sums[:, None, :], 0.0), axis=0)
    return (block_top.reshape(-1), total.reshape(-1))


def row_partial(tiles, rows_blk, cols_blk, valid, target_pot, row_blocks):
    width = tiles.shape[-1]
    pieces = target_pot.reshape(-1, width)[cols_blk]
    score = pieces[:, None, :] - tiles.astype(jnp.float32)
    slot_top = jnp.max(score, axis=2)

    def row_summed(own_top):
        return jnp.sum(jnp.exp(score - own_top[:, :, None]), axis=2)

    return block_reduce(slot_top, row_summed, rows_blk, row_blocks, valid)


def col_partial(tiles, rows_blk, cols_blk, valid, source_pot, col_blocks):
    width = tiles.shape[-1]
    pieces = source_pot.reshape(-1, width)[rows_blk]
    score = pieces[:, :, None] - tiles.astype(jnp.float32)
    slot_top = jnp.max(score, axis=1)

    def col_summed(own_top):
        return jnp.sum(jnp.exp(score - own_top[:, None, :]), axis=1)

    return block_reduce(slot_top, col_summed, cols_blk, col_blocks, valid)


def per_device(costs, block_rows, block_cols, live, log_source, log_target):
    tiles = costs[0, 0]
    rows_blk = block_rows[0, 0]
    cols_blk = block_cols[0, 0]
    count = live[0, 0]
    width = tiles.shape[-1]
    valid = jnp.arange(tiles.shape[0], dtype=jnp.int32) < count
    src_len = log_source.shape[0]
    tgt_len = log_target.shape[0]
    row_blocks = src_len // width
    col_blocks = tgt_len // width
    target_pot = jnp.zeros((tgt_len,), jnp.float32)
    source_pot = jnp.zeros((src_len,), jnp.float32)
    for sweep in range(ITERS):
        top, total = row_partial(tiles, rows_blk, cols_blk, valid, target_pot, row_blocks)
        common = lax.pmax(top, "cols")
        total = lax.psum(total * jnp.exp(top - common), "cols")
        top = common
        source_pot = log_source - (top + jnp.log(total))
        col_top, col_tot = col_partial(tiles, rows_blk, cols_blk, valid, source_pot, col_blocks)
        col_top, col_tot = combined_all((col_top, col_tot), "rows", combine)
        target_pot = log_target - (col_top + jnp.log(col_tot))
    return (source_pot, target_pot)


def solution(mesh):
    in_specs = (
        P("rows", "cols", None, None, None),
        P("rows", "cols", None),
        P("rows", "cols", None),
        P("rows", "cols"),
        P("rows"),
        P("cols"),
    )
    out_specs = (P("rows"), P("cols"))
    return jax.shard_map(
        per_device, mesh=mesh, in_specs=in_specs, out_specs=out_specs, check_vma=False
    )
```

profile of v0, /device:TPU:0, one launch (start us, length us, event | category | flops | bytes accessed | tf_op | source)
XLA Modules:
  0.0 195.3 jit_solution(16827550042038354003)
XLA Ops:
  1.4 0.9 fusion.24
  2.3 0.7 fusion.26
  3.0 0.6 gather_fusion
  3.6 2.8 %fusion.1 = f32[24,256]{1,0:T(8,128)S(1)} fusion(bf16[1,1,24,256,256]{4,3,2,1,0:T(8,128)(2,1)} %param.12, f32[24,256]{1,0:T(8,128)S(1)} %gather_fusion), kind=kLoop, calls=%fused_computation.22 | loop fusion | flops 4712448 | bytes 3194880 | tf_op jit(solution)/shard_map/reduce_max | solution.py:44
  6.7 2.1 %fusion.23 = f32[24,256]{1,0:T(8,128)S(1)} fusion(bf16[1,1,24,256,256]{4,3,2,1,0:T(8,128)(2,1)S(1)} %copy-done, f32[24,256]{1,0:T(8,128)S(1)} %broadcast_select_fusion.11, f32[24,256]{1,0:T(8,128)S(1)} %gather_fusion), kind=kLoop, calls=%fused_computation.44 | loop fusion | flops 6285312 | bytes 3219456 | tf_op jit(solution)/shard_map/reduce_sum | solution.py:47
  9.0 23.4 %pmax.21 = f32[2048]{0:T(1024)S(1)} all-reduce(f32[2048]{0:T(1024)S(1)} %bitcast.98), channel_id=1, replica_groups=mesh['rows'=4,'cols'=8] {'cols'}, use_global_device_ids=true, to_apply=%region_2.3 | all-reduce | flops 2048 | bytes 16384 | tf_op jit(solution)/shard_map/pmax | solution.py:79
  32.4 17.4 %psum.21 = f32[2048]{0:T(1024)S(1)} all-reduce(f32[2048]{0:T(1024)S(1)} %exponential_multiply_fusion.2), channel_id=1, replica_groups=mesh['rows'=4,'cols'=8] {'cols'}, use_global_device_ids=true, to_apply=%region_6.7 | all-reduce | flops 2048 | bytes 16384 | tf_op jit(solution)/shard_map/psum | solution.py:80
  49.9 0.6 gather_fusion.1
  50.5 1.0 fusion.3
  51.6 0.3 select_reduce_fusion.8
  51.9 0.3 select_reduce_fusion.7
  52.4 1.6 fusion.21
  54.0 0.3 select_reduce_fusion.6
  54.4 5.8 %all-gather.1 = f32[4,1,16384]{2,1,0:T(1,128)S(1)} all-gather(f32[1,1,16384]{2,1,0:T(1,128)S(1)} %reshape.438), channel_id=1, replica_groups=mesh['rows'=4,'cols'=8] {'rows'}, dimensions={0}, use_global_device_ids=true | all-gather | bytes 327680 | tf_op jit(solution)/shard_map/all_gather | solution.py:13
  60.2 0.2 copy.30
  60.4 0.7 reshape.436
  61.0 6.0 %all-gather = f32[4,1,16384]{2,1,0:T(1,128)S(1)} all-gather(f32[1,1,16384]{2,1,0:T(1,128)} %reshape.436), channel_id=1, replica_groups=mesh['rows'=4,'cols'=8] {'rows'}, dimensions={0}, use_global_device_ids=true | all-gather | bytes 327680 | tf_op jit(solution)/shard_map/all_gather | solution.py:13
  67.1 0.9 copy.31
  68.0 3.6 %while.51 = (s32[]{:T(128)}, f32[16384]{0:T(1024)S(1)}, f32[16384]{0:T(1024)S(1)}, f32[4,16384]{1,0:T(4,128)}, f32[4,16384]{1,0:T(4,128)S(1)}, /*index=5*/s32[]{:T(128)}, s32[]{:T(128)}, s32[]{:T(128)}) while((s32[]{:T(128)}, f32[16384]{0:T(1024)S(1)}, f32[16384]{0:T(1024)S(1)}, f32[4,16384]{1,0:T(4,128)}, f32[4,16384]{1,0:T(4,128)S(1)}, ...), condition=%wide.region_13.14_spmd, body=%wide.region_12.13_spmd.sunk | while | flops 98309 | bytes 655491 | solution.py:19
  68.0 1.1 constant_dynamic-slice_fusion.9
  69.2 1.1 constant_dynamic-slice_fusion.9
  70.4 1.1 constant_dynamic-slice_fusion.9
  71.6 0.9 add_subtract_fusion.2
  72.5 0.6 gather_fusion.2
  73.1 1.0 fusion.5
  74.4 2.1 %fusion.19 = f32[24,256]{1,0:T(8,128)S(1)} fusion(bf16[1,1,24,256,256]{4,3,2,1,0:T(8,128)(2,1)S(1)} %copy-done, f32[24,256]{1,0:T(8,128)S(1)} %broadcast_select_fusion.7, f32[24,256]{1,0:T(8,128)S(1)} %gather_fusion.2), kind=kLoop, calls=%fused_computation.40 | loop fusion | flops 6285312 | bytes 3219456 | tf_op jit(solution)/shard_map/reduce_sum | solution.py:47
  76.7 19.4 %pmax.22 = f32[2048]{0:T(1024)S(1)} all-reduce(f32[2048]{0:T(1024)S(1)} %bitcast.100), channel_id=1, replica_groups=mesh['rows'=4,'cols'=8] {'cols'}, use_global_device_ids=true, to_apply=%region_16.17 | all-reduce | flops 2048 | bytes 16384 | tf_op jit(solution)/shard_map/pmax | solution.py:79
  96.1 17.4 %psum.22 = f32[2048]{0:T(1024)S(1)} all-reduce(f32[2048]{0:T(1024)S(1)} %exponential_multiply_fusion.1), channel_id=1, replica_groups=mesh['rows'=4,'cols'=8] {'cols'}, use_global_device_ids=true, to_apply=%region_20.21 | all-reduce | flops 2048 | bytes 16384 | tf_op jit(solution)/shard_map/psum | solution.py:80
  113.5 0.7 gather_fusion.3
  114.2 1.0 fusion.7
  115.3 0.3 select_reduce_fusion.5
  115.5 0.3 select_reduce_fusion.4
  116.0 1.6 fusion.17
  117.6 0.3 select_reduce_fusion.3
  118.0 5.8 %all-gather.3 = f32[4,1,16384]{2,1,0:T(1,128)S(1)} all-gather(f32[1,1,16384]{2,1,0:T(1,128)S(1)} %reshape.442), channel_id=1, replica_groups=mesh['rows'=4,'cols'=8] {'rows'}, dimensions={0}, use_global_device_ids=true | all-gather | bytes 327680 | tf_op jit(solution)/shard_map/all_gather | solution.py:13
  123.8 0.2 copy.28
  124.0 0.7 reshape.440
  124.7 6.2 %all-gather.2 = f32[4,1,16384]{2,1,0:T(1,128)S(1)} all-gather(f32[1,1,16384]{2,1,0:T(1,128)} %reshape.440), channel_id=1, replica_groups=mesh['rows'=4,'cols'=8] {'rows'}, dimensions={0}, use_global_device_ids=true | all-gather | bytes 327680 | tf_op jit(solution)/shard_map/all_gather | solution.py:13
  130.9 0.9 copy.29
  131.8 3.6 %while.52 = (s32[]{:T(128)}, f32[16384]{0:T(1024)S(1)}, f32[16384]{0:T(1024)S(1)}, f32[4,16384]{1,0:T(4,128)}, f32[4,16384]{1,0:T(4,128)S(1)}, /*index=5*/s32[]{:T(128)}, s32[]{:T(128)}, s32[]{:T(128)}) while((s32[]{:T(128)}, f32[16384]{0:T(1024)S(1)}, f32[16384]{0:T(1024)S(1)}, f32[4,16384]{1,0:T(4,128)}, f32[4,16384]{1,0:T(4,128)S(1)}, ...), condition=%wide.region_27.28_spmd, body=%wide.region_26.27_spmd.sunk | while | flops 98309 | bytes 655491 | solution.py:19
  131.8 1.1 constant_dynamic-slice_fusion.10
  132.9 1.1 constant_dynamic-slice_fusion.10
  134.2 1.1 constant_dynamic-slice_fusion.10
  135.3 0.9 add_subtract_fusion.1
  136.2 0.6 gather_fusion.4
  136.8 1.0 fusion.9
  138.2 2.1 %fusion.15 = f32[24,256]{1,0:T(8,128)S(1)} fusion(bf16[1,1,24,256,256]{4,3,2,1,0:T(8,128)(2,1)S(1)} %copy-done, f32[24,256]{1,0:T(8,128)S(1)} %broadcast_select_fusion.3, f32[24,256]{1,0:T(8,128)S(1)} %gather_fusion.4), kind=kLoop, calls=%fused_computation.36 | loop fusion | flops 6285312 | bytes 3219456 | tf_op jit(solution)/shard_map/reduce_sum | solution.py:47
  140.4 19.4 %pmax.23 = f32[2048]{0:T(1024)S(1)} all-reduce(f32[2048]{0:T(1024)S(1)} %bitcast.102), channel_id=1, replica_groups=mesh['rows'=4,'cols'=8] {'cols'}, use_global_device_ids=true, to_apply=%region_30.31 | all-reduce | flops 2048 | bytes 16384 | tf_op jit(solution)/shard_map/pmax | solution.py:79
  159.9 17.4 %psum.23 = f32[2048]{0:T(1024)S(1)} all-reduce(f32[2048]{0:T(1024)S(1)} %exponential_multiply_fusion), channel_id=1, replica_groups=mesh['rows'=4,'cols'=8] {'cols'}, use_global_device_ids=true, to_apply=%region_34.35 | all-reduce | flops 2048 | bytes 16384 | tf_op jit(solution)/shard_map/psum | solution.py:80
  177.3 0.7 gather_fusion.5
  178.0 1.0 fusion.11
  179.1 0.3 select_reduce_fusion.2
  179.3 0.3 select_reduce_fusion.1
  179.8 1.6 fusion.13
  181.5 0.3 select_reduce_fusion
  181.8 5.8 %all-gather.5 = f32[4,1,16384]{2,1,0:T(1,128)S(1)} all-gather(f32[1,1,16384]{2,1,0:T(1,128)S(1)} %reshape.446), channel_id=1, replica_groups=mesh['rows'=4,'cols'=8] {'rows'}, dimensions={0}, use_global_device_ids=true | all-gather | bytes 327680 | tf_op jit(solution)/shard_map/all_gather | solution.py:13
  187.6 0.2 copy.26
  187.9 5.9 %all-gather.4 = f32[4,1,16384]{2,1,0:T(1,128)S(1)} all-gather(f32[1,1,16384]{2,1,0:T(1,128)S(1)} %reshape.444), channel_id=1, replica_groups=mesh['rows'=4,'cols'=8] {'rows'}, dimensions={0}, use_global_device_ids=true | all-gather | bytes 327680 | tf_op jit(solution)/shard_map/all_gather | solution.py:13
  193.7 0.2 copy.27
  193.9 0.7 while.53
  193.9 0.1 constant_dynamic-slice_fusion.11
  194.1 0.1 constant_dynamic-slice_fusion.11
  194.4 0.1 constant_dynamic-slice_fusion.11
  194.6 0.6 add_subtract_fusion
  (81 shorter events, 3.1 us)
Async XLA Ops:
  0.6 6.1 %copy-start = (bf16[1,1,24,256,256]{4,3,2,1,0:T(8,128)(2,1)S(1)}, bf16[1,1,24,256,256]{4,3,2,1,0:T(8,128)(2,1)}, u32[]{:S(2)}) copy-start(bf16[1,1,24,256,256]{4,3,2,1,0:T(8,128)(2,1)} %param.12) | copy-start | bytes 9437188
  3.6 46.2 %copy-start.2 = (f32[2048]{0:T(1024)S(1)}, f32[2048]{0:T(1024)}, u32[]{:S(2)}) copy-start(f32[2048]{0:T(1024)} %param.16) | copy-start | bytes 24580
  3.6 46.3 %copy-start.7 = (s32[1,1,24]{2,1,0:T(1,128)S(1)}, s32[1,1,24]{2,1,0:T(1,128)}, u32[]{:S(2)}) copy-start(s32[1,1,24]{2,1,0:T(1,128)} %param.13) | copy-start | bytes 292
  6.7 44.8 %copy-start.8 = (s32[1,1,24]{2,1,0:T(1,128)S(1)}, s32[1,1,24]{2,1,0:T(1,128)}, u32[]{:S(2)}) copy-start(s32[1,1,24]{2,1,0:T(1,128)} %param.14) | copy-start | bytes 292
  49.9 1.7 copy-start.6
  73.0 40.4 %copy-start.3 = (f32[2048]{0:T(1024)S(1)}, f32[2048]{0:T(1024)}, u32[]{:S(2)}) copy-start(f32[2048]{0:T(1024)} %param.16) | copy-start | bytes 24580
  136.8 40.4 %copy-start.4 = (f32[2048]{0:T(1024)S(1)}, f32[2048]{0:T(1024)}, u32[]{:S(2)}) copy-start(f32[2048]{0:T(1024)} %param.16) | copy-start | bytes 24580
  177.3 4.1 %copy-start.5 = (f32[2048]{0:T(1024)}, f32[2048]{0:T(1024)S(1)}, u32[]{:S(2)}) copy-start(f32[2048]{0:T(1024)S(1)} %add_subtract_fusion.3) | copy-start | bytes 24580
  181.4 13.2 %copy-start.1 = (f32[16384]{0:T(1024)S(1)}, f32[16384]{0:T(1024)}, u32[]{:S(2)}) copy-start(f32[16384]{0:T(1024)} %param.17) | copy-start | bytes 196612
where the time goes:
time: 196 us; the launch traced here: 195 us
  blocking collectives  150 us (77%)
  other arithmetic  28.1 us (14%)
  local copies, waits for them, and re-layouts  15.1 us (8%)
  between operations  2.1 us (1%)
    pmax x3, blocking collectives, per_device(): common = lax.pmax(top, 'cols')  62.2 us
    psum x3, blocking collectives, per_device(): total = lax.psum(total * jnp.exp(top - common), 'cols')  52.1 us
    all_gather x6, blocking collectives, combined_all(): everything = jax.tree.map(lambda part: lax.all_gather(part, axis), value)  35.5 us
    dynamic_slice x9, local copies, waits for them, and re-layouts, hop(): return combine(so_far, jax.tree.map(lambda part: part[k], everything))  7.07 us
    reduce_sum x3, other arithmetic, row_summed(): return jnp.sum(jnp.exp(score - own_top[:, :, None]), axis=2)  6.26 us
    reduce_sum x3, other arithmetic, col_summed(): return jnp.sum(jnp.exp(score - own_top[:, None, :]), axis=1)  4.79 us
    reduce_max x3, other arithmetic, row_partial(): slot_top = jnp.max(score, axis=2)  4.78 us
    unnamed x36, local copies, waits for them, and re-layouts  4.16 us

commit v1 on v0

v1 whole, which is shorter than its diff:
```python
import functools

import jax
import jax.numpy as jnp
from jax import lax
from jax.experimental import pallas as pl
from jax.experimental.pallas import tpu as pltpu
from jax.sharding import PartitionSpec as P

ITERS = 3
NEG = -1e30
LANES = 128
GROUP = 8
MESH = pl.DeviceIdType.MESH


def kernel(
    n_rows, n_cols,
    brows, bcols, live, costs, log_src, log_tgt,
    src_out, tgt_out,
    tiles, tiles_t, rid, cid, slot_top, slot_tot, part_src, src_col, piece, lt_piece,
    cid_all, src_buf, tgt_buf,
    load_sem, cid_send, cid_recv, src_send, src_recv, tgt_send, tgt_recv,
):
    slots, bs, _ = tiles.shape
    halves = bs // LANES
    row_blocks = part_src.shape[0]
    col_blocks = tgt_out.shape[0] // halves
    my_r = lax.axis_index("rows")
    my_c = lax.axis_index("cols")

    barrier = pltpu.get_barrier_semaphore()
    for k in range(1, n_rows):
        pl.semaphore_signal(barrier, inc=1, device_id=(lax.rem(my_r + k, n_rows), my_c), device_id_type=MESH)
    for k in range(1, n_cols):
        pl.semaphore_signal(barrier, inc=1, device_id=(my_r, lax.rem(my_c + k, n_cols)), device_id_type=MESH)

    loads = []
    for c in range(slots // GROUP):
        part = pl.ds(c * GROUP, GROUP)
        loads.append(pltpu.make_async_copy(costs.at[part], tiles.at[part], load_sem.at[c]))
        loads[-1].start()

    count = live[0]
    for t in range(slots):
        okay = t < count
        rid[t : t + 1, :] = jnp.full((1, LANES), jnp.where(okay, brows[t], -1), jnp.int32)
        cid[t : t + 1, :] = jnp.full((1, LANES), jnp.where(okay, bcols[t], -1), jnp.int32)
    wide_cid = cid[...]
    cid_all[pl.ds(my_r, 1)] = wide_cid[None]

    def send(k, along, src, dst, send_sem, recv_sem):
        if along == "rows":
            peer = (lax.rem(my_r + k, n_rows), my_c)
        else:
            peer = (my_r, lax.rem(my_c + k, n_cols))
        return pltpu.make_async_remote_copy(
            src_ref=src, dst_ref=dst, send_sem=send_sem, recv_sem=recv_sem,
            device_id=peer, device_id_type=MESH)

    def exchange(along, n, me, src, buf, send_sem, recv_sem):
        outs = [send(k, along, src, buf.at[me], send_sem.at[k], recv_sem.at[k]) for k in range(1, n)]
        for copy in outs:
            copy.start()
        return outs

    def arrived(along, n, me, src, buf, send_sem, recv_sem):
        for k in range(1, n):
            frm = lax.rem(me + n - k, n)
            send(k, along, src, buf.at[frm], send_sem.at[k], recv_sem.at[k]).wait_recv()

    def group_lse(g, col, tile):
        tops, tots = [], []
        for i in range(GROUP):
            t = g * GROUP + i
            column = col(t, i)
            top_h, tot_h = [], []
            for h in range(halves):
                lanes = slice(h * LANES, (h + 1) * LANES)
                score = -tile(t, lanes) if column is None else column - tile(t, lanes)
                top = jnp.max(score, axis=0, keepdims=True)
                top_h.append(top)
                tot_h.append(jnp.sum(jnp.exp(score - top), axis=0, keepdims=True))
            tops.append(jnp.concatenate(top_h, axis=1))
            tots.append(jnp.concatenate(tot_h, axis=1))
        at = pl.ds(pl.multiple_of(g * GROUP, GROUP), GROUP)
        slot_top[at, :] = jnp.concatenate(tops, axis=0)
        slot_tot[at, :] = jnp.concatenate(tots, axis=0)

    def slot_lse(ids):
        ok = jnp.concatenate([ids] * halves, axis=1) >= 0
        return jnp.where(ok, slot_top[...] + jnp.log(slot_tot[...]), NEG)

    def as_column(row):
        return jnp.concatenate(
            [jnp.broadcast_to(row[:, h * LANES : (h + 1) * LANES], (LANES, LANES)).T for h in range(halves)], axis=0)

    eye = (lax.broadcasted_iota(jnp.int32, (bs, bs), 0) == lax.broadcasted_iota(jnp.int32, (bs, bs), 1))
    eye = eye.astype(jnp.float32).astype(jnp.bfloat16)
    for c in range(slots // GROUP):
        loads[c].wait()

        def turn(t, _):
            tiles_t[t] = lax.dot_general(eye, tiles[t], (((1,), (1,)), ((), ())), preferred_element_type=jnp.float32)
            return 0

        lax.fori_loop(c * GROUP, (c + 1) * GROUP, turn, 0, unroll=2)
        group_lse(c, lambda t, i: None, lambda t, lanes: tiles_t[t, :, lanes])

    pl.semaphore_wait(barrier, n_rows + n_cols - 2)
    cid_copies = exchange("rows", n_rows, my_r, cid, cid_all, cid_send, cid_recv)

    for t in range(slots):
        col_at = bcols[t] * halves
        for h in range(halves):
            lt_piece[t : t + 1, h * LANES : (h + 1) * LANES] = log_tgt[pl.ds(col_at + h, 1), :]
    ls = jnp.concatenate([log_src[pl.ds(h, row_blocks, stride=halves), :] for h in range(halves)], axis=1)

    def wide(mask):
        return jnp.concatenate([mask] * halves, axis=1)

    waits = list(cid_copies)
    block_of = lax.broadcasted_iota(jnp.int32, (row_blocks, LANES), 0)
    for sweep in range(ITERS):
        if sweep:
            def row_group(g, _):
                rows = piece[pl.ds(pl.multiple_of(g * GROUP, GROUP), GROUP), :]
                group_lse(g, lambda t, i: as_column(rows[i : i + 1]), lambda t, lanes: tiles_t[t, :, lanes])
                return 0

            lax.fori_loop(0, slots // GROUP, row_group, 0)
        slot_top[...] = slot_lse(rid[...])
        top = jnp.full((row_blocks, bs), NEG, jnp.float32)
        for t in range(slots):
            here = wide(block_of == rid[t : t + 1, :])
            top = jnp.maximum(top, jnp.where(here, slot_top[t : t + 1, :], NEG))
        total = jnp.zeros((row_blocks, bs), jnp.float32)
        for t in range(slots):
            here = wide(block_of == rid[t : t + 1, :])
            total = total + jnp.exp(jnp.where(here, slot_top[t : t + 1, :], NEG) - top)
        part_src[...] = top + jnp.log(total)
        s_buf = src_buf.at[sweep]
        s_send, s_recv = src_send.at[sweep], src_recv.at[sweep]
        mine = exchange("cols", n_cols, my_c, part_src, s_buf, s_send, s_recv)
        s_buf[pl.ds(my_c, 1)] = part_src[...][None]
        arrived("cols", n_cols, my_c, part_src, s_buf, s_send, s_recv)
        top = s_buf[0]
        for k in range(1, n_cols):
            top = jnp.maximum(top, s_buf[k])
        total = jnp.exp(s_buf[0] - top)
        for k in range(1, n_cols):
            total = total + jnp.exp(s_buf[k] - top)
        source = ls - (top + jnp.log(total))
        for copy in mine:
            copy.wait_send()
        for b in range(row_blocks):
            src_col[b] = as_column(source[b : b + 1, :])

        def col_group(g, _):
            group_lse(g, lambda t, i: src_col[brows[t]], lambda t, lanes: tiles[t, :, lanes].astype(jnp.float32))
            return 0

        lax.fori_loop(0, slots // GROUP, col_group, 0)
        if sweep == 0:
            arrived("rows", n_rows, my_r, cid, cid_all, cid_send, cid_recv)
        t_buf = tgt_buf.at[sweep]
        t_send, t_recv = tgt_send.at[sweep], tgt_recv.at[sweep]
        slot_top[...] = slot_lse(cid[...])
        mine = exchange("rows", n_rows, my_r, slot_top, t_buf, t_send, t_recv)
        t_buf[pl.ds(my_r, 1)] = slot_top[...][None]
        arrived("rows", n_rows, my_r, slot_top, t_buf, t_send, t_recv)
        last = sweep == ITERS - 1
        if last:
            ids = lax.broadcasted_iota(jnp.int32, (col_blocks, LANES), 0)
        else:
            ids = cid[...]

        def gather_lse(ids):
            def each(g):
                at = pl.ds(pl.multiple_of(g * GROUP, GROUP), GROUP)
                for r in range(n_rows):
                    theirs, found = cid_all[r, at, :], t_buf[r, at, :]
                    for i in range(GROUP):
                        here = wide(ids == theirs[i : i + 1])
                        yield jnp.where(here, found[i : i + 1], NEG)

            def top_of(g, top):
                for value in each(g):
                    top = jnp.maximum(top, value)
                return top

            shape = (ids.shape[0], bs)
            top = lax.fori_loop(0, slots // GROUP, top_of, jnp.full(shape, NEG, jnp.float32))

            def total_of(g, total):
                for value in each(g):
                    total = total + jnp.exp(value - top)
                return total

            total = lax.fori_loop(0, slots // GROUP, total_of, jnp.zeros(shape, jnp.float32))
            return top + jnp.log(total)

        if not last:
            piece[...] = jnp.where(wide(ids >= 0), lt_piece[...] - gather_lse(ids), 0.0)
        else:
            per = 16 if col_blocks % 16 == 0 else col_blocks
            for b in range(0, col_blocks, per):
                part = ids[b : b + per]
                found = gather_lse(part)
                for h in range(halves):
                    rows = pl.ds(b * halves + h, per, stride=halves)
                    tgt_out[rows, :] = log_tgt[rows, :] - found[:, h * LANES : (h + 1) * LANES]
            for h in range(halves):
                src_out[pl.ds(h, row_blocks, stride=halves), :] = source[:, h * LANES : (h + 1) * LANES]
        for copy in mine:
            copy.wait_send()
    for copy in waits:
        copy.wait_send()


def per_device(n_rows, n_cols, costs, block_rows, block_cols, live, log_source, log_target):
    tiles = costs[0, 0]
    slots, bs, _ = tiles.shape
    src_rows = log_source.shape[0] // LANES
    tgt_rows = log_target.shape[0] // LANES
    row_blocks = log_source.shape[0] // bs
    f32 = jnp.float32
    dma = pltpu.SemaphoreType.DMA
    smem = pl.BlockSpec(memory_space=pltpu.SMEM)
    vmem = pl.BlockSpec(memory_space=pltpu.VMEM)
    source, target = pl.pallas_call(
        functools.partial(kernel, n_rows, n_cols),
        out_shape=(jax.ShapeDtypeStruct((src_rows, LANES), f32), jax.ShapeDtypeStruct((tgt_rows, LANES), f32)),
        in_specs=[smem, smem, smem, pl.BlockSpec(memory_space=pl.ANY), vmem, vmem],
        out_specs=(vmem, vmem),
        scratch_shapes=[
            pltpu.VMEM((slots, bs, bs), tiles.dtype),
            pltpu.VMEM((slots, bs, bs), f32),
            pltpu.VMEM((slots, LANES), jnp.int32),
            pltpu.VMEM((slots, LANES), jnp.int32),
            pltpu.VMEM((slots, bs), f32),
            pltpu.VMEM((slots, bs), f32),
            pltpu.VMEM((row_blocks, bs), f32),
            pltpu.VMEM((row_blocks, bs, LANES), f32),
            pltpu.VMEM((slots, bs), f32),
            pltpu.VMEM((slots, bs), f32),
            pltpu.VMEM((n_rows, slots, LANES), jnp.int32),
            pltpu.VMEM((ITERS, n_cols, row_blocks, bs), f32),
            pltpu.VMEM((ITERS, n_rows, slots, bs), f32),
            dma((slots // GROUP,)),
            dma((n_rows,)), dma((n_rows,)),
            dma((ITERS, n_cols)), dma((ITERS, n_cols)),
            dma((ITERS, n_rows)), dma((ITERS, n_rows)),
        ],
        compiler_params=pltpu.CompilerParams(collective_id=0, has_side_effects=True),
    )(
        block_rows.reshape(-1), block_cols.reshape(-1), live.reshape(-1), tiles,
        log_source.reshape(src_rows, LANES), log_target.reshape(tgt_rows, LANES),
    )
    return source.reshape(-1), target.reshape(-1)


def solution(mesh):
    in_specs = (
        P("rows", "cols", None, None, None),
        P("rows", "cols", None),
        P("rows", "cols", None),
        P("rows", "cols"),
        P("rows"),
        P("cols"),
    )
    out_specs = (P("rows"), P("cols"))
    body = functools.partial(per_device, mesh.shape["rows"], mesh.shape["cols"])
    return jax.shard_map(body, mesh=mesh, in_specs=in_specs, out_specs=out_specs, check_vma=False)
```

time: 196 us -> 50.5 us (0.26)
  blocking collectives: 150 us -> 0 us
  Pallas kernels: 0 us -> 46.2 us
  other arithmetic: 28.1 us -> 0 us
  local copies, waits for them, and re-layouts: 15.1 us -> 2.77 us
    pmax x3 -> x0, blocking collectives: 62.2 us -> none  [per_device(): common = lax.pmax(top, 'cols')]
    psum x3 -> x0, blocking collectives: 52.1 us -> none  [per_device(): total = lax.psum(total * jnp.exp(top - common), 'cols')]
    pallas_call x0 -> x1, Pallas kernels: none -> 46.2 us  [per_device(): pl.pallas_call(functools.partial(kernel, n_rows, n_cols), out_shape=(jax....]
    all_gather x6 -> x0, blocking collectives: 35.5 us -> none  [combined_all(): everything = jax.tree.map(lambda part: lax.all_gather(part, axis), value)]
    reduce_sum x12 -> x0, other arithmetic: 12.1 us -> none  [the longest x3 6.26 us: row_summed(): return jnp.sum(jnp.exp(score - own_top[:, :, None]), axis=2)]
    reduce_max x18 -> x0, other arithmetic: 10.4 us -> none  [the longest x3 4.78 us: row_partial(): slot_top = jnp.max(score, axis=2)]
    dynamic_slice x9 -> x0, local copies, waits for them, and re-layouts: 7.07 us -> none  [hop(): return combine(so_far, jax.tree.map(lambda part: part[k], everything))]
    gather x6 -> x0, local copies, waits for them, and re-layouts: 3.78 us -> none  [the longest x3 2.01 us: col_partial(): pieces = source_pot.reshape(-1, width)[rows_blk]]
where the time goes in v1:
time: 50.5 us; the launch traced here: 50.3 us
  Pallas kernels  46.2 us (91%)
  local copies, waits for them, and re-layouts  2.77 us (5%)
  between operations  1.29 us (3%)
    pallas_call x1, Pallas kernels, per_device(): pl.pallas_call(functools.partial(kernel, n_rows, n_cols), out_shape=(jax....  46.2 us
    unnamed x2, local copies, waits for them, and re-layouts  2.77 us

profile of v1, /device:TPU:0, one launch (start us, length us, event | category | flops | bytes accessed | tf_op | source)
XLA Modules:
  0.0 50.3 jit_solution(9302614693853009907)
XLA Ops:
  1.3 46.2 %shard_map.77 = (f32[16,128]{1,0:T(8,128)}, f32[128,128]{1,0:T(8,128)}) custom-call(s32[24]{0:T(128)} %bitcast.14, s32[24]{0:T(128)} %bitcast.15, s32[1]{0:T(128)} %bitcast.8.live, bf16[24,256,256]{2,1,0:T(8,128)(2,1)} %bitcast.9, f32[16,128]{1,0:T(8,128)} %bitcast.12, f32[128,128]{1,0:T(8,128)} %bitcast.10), custom_call_target="tpu_custom_call" | custom-call | tf_op jit(solution)/shard_map/pallas_call | solution.py:231
  47.5 1.3 %copy.11 = f32[2048]{0:T(1024)} copy(f32[2048]{0:T(1024)} %bitcast.13) | data formatting | bytes 16384
  48.8 1.5 %copy.12 = f32[16384]{0:T(1024)} copy(f32[16384]{0:T(1024)} %bitcast.11) | data formatting | bytes 131072

commit v2 on v1

--- a/solution.py
+++ b/solution.py
@@ -9,23 +9,28 @@
 
 ITERS = 3
 NEG = -1e30
+LOG2E = 1.4426950408889634
+LN2 = 0.6931471805599453
 LANES = 128
 GROUP = 8
 MESH = pl.DeviceIdType.MESH
 
 
+def log2(x):
+    return jnp.log(x) * LOG2E
+
+
 def kernel(
     n_rows, n_cols,
     brows, bcols, live, costs, log_src, log_tgt,
-    src_out, tgt_out,
-    tiles, tiles_t, rid, cid, slot_top, slot_tot, part_src, src_col, piece, lt_piece,
+    src_out, lse_out, ids_out,
+    tiles, tiles_s, tiles_t, rid, cid, slot_top, slot_tot, part_src, src_col, piece, lt_piece,
     cid_all, src_buf, tgt_buf,
     load_sem, cid_send, cid_recv, src_send, src_recv, tgt_send, tgt_recv,
 ):
     slots, bs, _ = tiles.shape
     halves = bs // LANES
     row_blocks = part_src.shape[0]
-    col_blocks = tgt_out.shape[0] // halves
     my_r = lax.axis_index("rows")
     my_c = lax.axis_index("cols")
 
@@ -80,7 +85,7 @@
                 score = -tile(t, lanes) if column is None else column - tile(t, lanes)
                 top = jnp.max(score, axis=0, keepdims=True)
                 top_h.append(top)
-                tot_h.append(jnp.sum(jnp.exp(score - top), axis=0, keepdims=True))
+                tot_h.append(jnp.sum(jnp.exp2(score - top), axis=0, keepdims=True))
             tops.append(jnp.concatenate(top_h, axis=1))
             tots.append(jnp.concatenate(tot_h, axis=1))
         at = pl.ds(pl.multiple_of(g * GROUP, GROUP), GROUP)
@@ -89,7 +94,7 @@
 
     def slot_lse(ids):
         ok = jnp.concatenate([ids] * halves, axis=1) >= 0
-        return jnp.where(ok, slot_top[...] + jnp.log(slot_tot[...]), NEG)
+        return jnp.where(ok, slot_top[...] + log2(slot_tot[...]), NEG)
 
     def as_column(row):
         return jnp.concatenate(
@@ -101,7 +106,10 @@
         loads[c].wait()
 
         def turn(t, _):
-            tiles_t[t] = lax.dot_general(eye, tiles[t], (((1,), (1,)), ((), ())), preferred_element_type=jnp.float32)
+            tile = tiles[t]
+            turned = lax.dot_general(eye, tile, (((1,), (1,)), ((), ())), preferred_element_type=jnp.float32)
+            tiles_t[t] = turned * LOG2E
+            tiles_s[t] = tile.astype(jnp.float32) * LOG2E
             return 0
 
         lax.fori_loop(c * GROUP, (c + 1) * GROUP, turn, 0, unroll=2)
@@ -113,8 +121,8 @@
     for t in range(slots):
         col_at = bcols[t] * halves
         for h in range(halves):
-            lt_piece[t : t + 1, h * LANES : (h + 1) * LANES] = log_tgt[pl.ds(col_at + h, 1), :]
-    ls = jnp.concatenate([log_src[pl.ds(h, row_blocks, stride=halves), :] for h in range(halves)], axis=1)
+            lt_piece[t : t + 1, h * LANES : (h + 1) * LANES] = log_tgt[pl.ds(col_at + h, 1), :] * LOG2E
+    ls = jnp.concatenate([log_src[pl.ds(h, row_blocks, stride=halves), :] * LOG2E for h in range(halves)], axis=1)
 
     def wide(mask):
         return jnp.concatenate([mask] * halves, axis=1)
@@ -137,8 +145,8 @@
         total = jnp.zeros((row_blocks, bs), jnp.float32)
         for t in range(slots):
             here = wide(block_of == rid[t : t + 1, :])
-            total = total + jnp.exp(jnp.where(here, slot_top[t : t + 1, :], NEG) - top)
-        part_src[...] = top + jnp.log(total)
+            total = total + jnp.exp2(jnp.where(here, slot_top[t : t + 1, :], NEG) - top)
+        part_src[...] = top + log2(total)
         s_buf = src_buf.at[sweep]
         s_send, s_recv = src_send.at[sweep], src_recv.at[sweep]
         mine = exchange("cols", n_cols, my_c, part_src, s_buf, s_send, s_recv)
@@ -147,17 +155,17 @@
         top = s_buf[0]
         for k in range(1, n_cols):
             top = jnp.maximum(top, s_buf[k])
-        total = jnp.exp(s_buf[0] - top)
+        total = jnp.exp2(s_buf[0] - top)
         for k in range(1, n_cols):
-            total = total + jnp.exp(s_buf[k] - top)
-        source = ls - (top + jnp.log(total))
+            total = total + jnp.exp2(s_buf[k] - top)
+        source = ls - (top + log2(total))
         for copy in mine:
             copy.wait_send()
         for b in range(row_blocks):
             src_col[b] = as_column(source[b : b + 1, :])
 
         def col_group(g, _):
-            group_lse(g, lambda t, i: src_col[brows[t]], lambda t, lanes: tiles[t, :, lanes].astype(jnp.float32))
+            group_lse(g, lambda t, i: src_col[brows[t]], lambda t, lanes: tiles_s[t, :, lanes])
             return 0
 
         lax.fori_loop(0, slots // GROUP, col_group, 0)
@@ -170,10 +178,6 @@
         t_buf[pl.ds(my_r, 1)] = slot_top[...][None]
         arrived("rows", n_rows, my_r, slot_top, t_buf, t_send, t_recv)
         last = sweep == ITERS - 1
-        if last:
-            ids = lax.broadcasted_iota(jnp.int32, (col_blocks, LANES), 0)
-        else:
-            ids = cid[...]
 
         def gather_lse(ids):
             def each(g):
@@ -194,28 +198,55 @@
 
             def total_of(g, total):
                 for value in each(g):
-                    total = total + jnp.exp(value - top)
+                    total = total + jnp.exp2(value - top)
                 return total
 
             total = lax.fori_loop(0, slots // GROUP, total_of, jnp.zeros(shape, jnp.float32))
-            return top + jnp.log(total)
+            return top + log2(total)
 
         if not last:
+            ids = cid[...]
             piece[...] = jnp.where(wide(ids >= 0), lt_piece[...] - gather_lse(ids), 0.0)
         else:
-            per = 16 if col_blocks % 16 == 0 else col_blocks
-            for b in range(0, col_blocks, per):
-                part = ids[b : b + per]
-                found = gather_lse(part)
-                for h in range(halves):
-                    rows = pl.ds(b * halves + h, per, stride=halves)
-                    tgt_out[rows, :] = log_tgt[rows, :] - found[:, h * LANES : (h + 1) * LANES]
-            for h in range(halves):
-                src_out[pl.ds(h, row_blocks, stride=halves), :] = source[:, h * LANES : (h + 1) * LANES]
+            for r in range(n_rows):
+                lse_out[r * slots : (r + 1) * slots, :] = t_buf[r]
+                ids_out[r * slots : (r + 1) * slots, :] = cid_all[r]
+            src_out[...] = source * LN2
         for copy in mine:
             copy.wait_send()
     for copy in waits:
         copy.wait_send()
+
+
+def final_kernel(source, lse, ids, log_tgt, src_out, tgt_out, top_buf):
+    found, bs = lse.shape
+    halves = bs // LANES
+    blocks = tgt_out.shape[0] // halves
+    exact = functools.partial(jnp.dot, preferred_element_type=jnp.float32, precision=lax.Precision.HIGHEST)
+    per = 16 if blocks % 16 == 0 else blocks
+    for b in range(0, blocks, per):
+        block = lax.broadcasted_iota(jnp.int32, (per, LANES), 0) + b
+
+        def top_of(g, top):
+            at = pl.ds(pl.multiple_of(g * GROUP, GROUP), GROUP)
+            theirs, values = ids[at, :], lse[at, :]
+            for i in range(GROUP):
+                here = jnp.concatenate([block == theirs[i : i + 1]] * halves, axis=1)
+                top = jnp.maximum(top, jnp.where(here, values[i : i + 1], NEG))
+            return top
+
+        top_buf[b : b + per, :] = lax.fori_loop(
+            0, found // GROUP, top_of, jnp.full((per, bs), NEG, jnp.float32), unroll=3 if found % (3 * GROUP) == 0 else 2)
+    top = top_buf[...]
+    names = ids[...].astype(jnp.float32)
+    back = (names[:, 0:1] == lax.broadcasted_iota(jnp.int32, (found, blocks), 1).astype(jnp.float32)).astype(jnp.float32)
+    into = (names.T[0:1, :] == lax.broadcasted_iota(jnp.int32, (blocks, found), 0).astype(jnp.float32)).astype(jnp.float32)
+    total = exact(into, jnp.exp2(lse[...] - exact(back, top)))
+    found_lse = top * LN2 + jnp.log(total)
+    for h in range(halves):
+        rows = pl.ds(h, blocks, stride=halves)
+        tgt_out[rows, :] = log_tgt[rows, :] - found_lse[:, h * LANES : (h + 1) * LANES]
+        src_out[pl.ds(h, source.shape[0], stride=halves), :] = source[:, h * LANES : (h + 1) * LANES]
 
 
 def per_device(n_rows, n_cols, costs, block_rows, block_cols, live, log_source, log_target):
@@ -228,13 +259,19 @@
     dma = pltpu.SemaphoreType.DMA
     smem = pl.BlockSpec(memory_space=pltpu.SMEM)
     vmem = pl.BlockSpec(memory_space=pltpu.VMEM)
-    source, target = pl.pallas_call(
+    found = n_rows * slots
+    source, lse, ids = pl.pallas_call(
         functools.partial(kernel, n_rows, n_cols),
-        out_shape=(jax.ShapeDtypeStruct((src_rows, LANES), f32), jax.ShapeDtypeStruct((tgt_rows, LANES), f32)),
+        out_shape=(
+            jax.ShapeDtypeStruct((row_blocks, bs), f32),
+            jax.ShapeDtypeStruct((found, bs), f32),
+            jax.ShapeDtypeStruct((found, LANES), jnp.int32),
+        ),
         in_specs=[smem, smem, smem, pl.BlockSpec(memory_space=pl.ANY), vmem, vmem],
-        out_specs=(vmem, vmem),
+        out_specs=(vmem, vmem, vmem),
         scratch_shapes=[
             pltpu.VMEM((slots, bs, bs), tiles.dtype),
+            pltpu.VMEM((slots, bs, bs), f32),
             pltpu.VMEM((slots, bs, bs), f32),
             pltpu.VMEM((slots, LANES), jnp.int32),
             pltpu.VMEM((slots, LANES), jnp.int32),
@@ -252,11 +289,19 @@
             dma((ITERS, n_cols)), dma((ITERS, n_cols)),
             dma((ITERS, n_rows)), dma((ITERS, n_rows)),
         ],
-        compiler_params=pltpu.CompilerParams(collective_id=0, has_side_effects=True),
+        compiler_params=pltpu.CompilerParams(collective_id=0, has_side_effects=True, vmem_limit_bytes=62 << 20),
     )(
         block_rows.reshape(-1), block_cols.reshape(-1), live.reshape(-1), tiles,
         log_source.reshape(src_rows, LANES), log_target.reshape(tgt_rows, LANES),
     )
+    source, target = pl.pallas_call(
+        final_kernel,
+        out_shape=(jax.ShapeDtypeStruct((src_rows, LANES), f32), jax.ShapeDtypeStruct((tgt_rows, LANES), f32)),
+        in_specs=[vmem] * 4,
+        out_specs=(vmem, vmem),
+        scratch_shapes=[pltpu.VMEM((tgt_rows * LANES // bs, bs), f32)],
+        compiler_params=pltpu.CompilerParams(vmem_limit_bytes=8 << 20),
+    )(source, lse, ids, log_target.reshape(tgt_rows, LANES))
     return source.reshape(-1), target.reshape(-1)
 
 

time: 50.5 us -> 49.5 us (0.980)
  Pallas kernels: 46.2 us -> 45.4 us
    pallas_call x1, Pallas kernels: 46.2 us -> 43.7 us  [per_device(): pl.pallas_call(functools.partial(kernel, n_rows, n_cols), out_shape=(jax....]
    pallas_call x0 -> x1, Pallas kernels: none -> 1.74 us  [per_device(): pl.pallas_call(final_kernel, out_shape=(jax.ShapeDtypeStruct((src_rows, L...]
    unnamed x2 -> x8, local copies, waits for them, and re-layouts: 2.77 us -> 2.38 us
where the time goes in v2:
time: 49.5 us; the launch traced here: 49.2 us
  Pallas kernels  45.4 us (92%)
  local copies, waits for them, and re-layouts  2.38 us (5%)
  between operations  1.34 us (3%)
    pallas_call x1, Pallas kernels, per_device(): pl.pallas_call(functools.partial(kernel, n_rows, n_cols), out_shape=(jax....  43.7 us
    unnamed x8, local copies, waits for them, and re-layouts  2.38 us
    pallas_call x1, Pallas kernels, per_device(): pl.pallas_call(final_kernel, out_shape=(jax.ShapeDtypeStruct((src_rows, L...  1.74 us

profile of v2, /device:TPU:0, one launch (start us, length us, event | category | flops | bytes accessed | tf_op | source)
XLA Modules:
  0.0 49.2 jit_solution(2939855712695379716)
XLA Ops:
  0.6 0.0 copy-start
  1.3 43.7 %shard_map.77 = (f32[8,256]{1,0:T(8,128)}, f32[96,256]{1,0:T(8,128)}, s32[96,128]{1,0:T(8,128)}) custom-call(s32[24]{0:T(128)} %bitcast.13, s32[24]{0:T(128)} %bitcast.14, s32[1]{0:T(128)} %bitcast.8.live, bf16[24,256,256]{2,1,0:T(8,128)(2,1)} %bitcast.11, f32[16,128]{1,0:T(8,128)} %bitcast.12, f32[128,128]{1,0:T(8,128)} %bitcast.9), custom_call_target="tpu_custom_call" | custom-call | tf_op jit(solution)/shard_map/pallas_call | solution.py:263
  45.0 0.0 copy-done
  45.0 0.0 copy-start.1
  45.0 0.9 %copy-done.1 = f32[96,256]{1,0:T(8,128)S(1)} copy-done((f32[96,256]{1,0:T(8,128)S(1)}, f32[96,256]{1,0:T(8,128)}, u32[]{:S(2)}) %copy-start.1) | copy-done | bytes 98328
  45.9 0.0 copy-start.2
  45.9 0.8 %copy-done.2 = s32[96,128]{1,0:T(8,128)S(1)} copy-done((s32[96,128]{1,0:T(8,128)S(1)}, s32[96,128]{1,0:T(8,128)}, u32[]{:S(2)}) %copy-start.2) | copy-done | bytes 49176
  46.7 0.0 copy-start.3
  46.7 0.7 %copy-done.3 = f32[8,256]{1,0:T(8,128)S(1)} copy-done((f32[8,256]{1,0:T(8,128)S(1)}, f32[8,256]{1,0:T(8,128)}, u32[]{:S(2)}) %copy-start.3) | copy-done | bytes 8216
  47.4 1.7 %shard_map.78 = (f32[16,128]{1,0:T(8,128)}, f32[128,128]{1,0:T(8,128)}) custom-call(f32[8,256]{1,0:T(8,128)S(1)} %copy-done.3, f32[96,256]{1,0:T(8,128)S(1)} %copy-done.1, s32[96,128]{1,0:T(8,128)S(1)} %copy-done.2, f32[128,128]{1,0:T(8,128)S(1)} %bitcast.10), custom_call_target="tpu_custom_call" | custom-call | tf_op jit(solution)/shard_map/pallas_call | solution.py:297
Async XLA Ops:
  0.6 44.4 %copy-start = (f32[16384]{0:T(1024)S(1)}, f32[16384]{0:T(1024)}, u32[]{:S(2)}) copy-start(f32[16384]{0:T(1024)} %param.11) | copy-start | bytes 196612
  45.0 0.9 %copy-start.1 = (f32[96,256]{1,0:T(8,128)S(1)}, f32[96,256]{1,0:T(8,128)}, u32[]{:S(2)}) copy-start(f32[96,256]{1,0:T(8,128)} %get-tuple-element.8.lse) | copy-start | bytes 294916
  45.9 0.8 %copy-start.2 = (s32[96,128]{1,0:T(8,128)S(1)}, s32[96,128]{1,0:T(8,128)}, u32[]{:S(2)}) copy-start(s32[96,128]{1,0:T(8,128)} %get-tuple-element.9.ids) | copy-start | bytes 147460
  46.7 0.7 %copy-start.3 = (f32[8,256]{1,0:T(8,128)S(1)}, f32[8,256]{1,0:T(8,128)}, u32[]{:S(2)}) copy-start(f32[8,256]{1,0:T(8,128)} %get-tuple-element.7.source) | copy-start | bytes 24580

commit v3 on v2

v3 whole, which is shorter than its diff:
```python
import functools

import jax
import jax.numpy as jnp
from jax import lax
from jax.experimental import pallas as pl
from jax.experimental.pallas import tpu as pltpu
from jax.sharding import PartitionSpec as P

ITERS = 3
NEG = -1e30
LOG2E = 1.4426950408889634
LN2 = 0.6931471805599453
LANES = 128
GROUP = 8
MESH = pl.DeviceIdType.MESH


def log2(x):
    return jnp.log(x) * LOG2E


def kernel(
    n_rows, n_cols,
    brows, bcols, live, costs, log_src, log_tgt,
    src_out, lse_out, ids_out,
    tiles, tiles_s, tiles_t, rid, cid, slot_top, slot_tot, part_src, part_tgt, columns, src_col, piece, lt_piece,
    cid_all, src_buf, tgt_buf,
    load_sem, cid_send, cid_recv, src_send, src_recv, tgt_send, tgt_recv,
):
    slots, bs, _ = tiles.shape
    halves = bs // LANES
    row_blocks = part_src.shape[1]
    my_r = lax.axis_index("rows")
    my_c = lax.axis_index("cols")

    barrier = pltpu.get_barrier_semaphore()
    for k in range(1, n_rows):
        pl.semaphore_signal(barrier, inc=1, device_id=(lax.rem(my_r + k, n_rows), my_c), device_id_type=MESH)
    for k in range(1, n_cols):
        pl.semaphore_signal(barrier, inc=1, device_id=(my_r, lax.rem(my_c + k, n_cols)), device_id_type=MESH)

    loads = []
    for c in range(slots // GROUP):
        part = pl.ds(c * GROUP, GROUP)
        loads.append(pltpu.make_async_copy(costs.at[part], tiles.at[part], load_sem.at[c]))
        loads[-1].start()

    count = live[0]
    for t in range(slots):
        okay = t < count
        rid[t : t + 1, :] = jnp.full((1, LANES), jnp.where(okay, brows[t], -1), jnp.int32)
        cid[t : t + 1, :] = jnp.full((1, LANES), jnp.where(okay, bcols[t], -1), jnp.int32)
    wide_cid = cid[...]
    cid_all[pl.ds(my_r, 1)] = wide_cid[None]

    def send(k, along, src, dst, send_sem, recv_sem):
        if along == "rows":
            peer = (lax.rem(my_r + k, n_rows), my_c)
        else:
            peer = (my_r, lax.rem(my_c + k, n_cols))
        return pltpu.make_async_remote_copy(
            src_ref=src, dst_ref=dst, send_sem=send_sem, recv_sem=recv_sem,
            device_id=peer, device_id_type=MESH)

    def exchange(along, n, me, src, buf, send_sem, recv_sem):
        outs = [send(k, along, src, buf.at[me], send_sem.at[k], recv_sem.at[k]) for k in range(1, n)]
        for copy in outs:
            copy.start()
        return outs

    def arrived(along, n, me, src, buf, send_sem, recv_sem):
        for k in range(1, n):
            frm = lax.rem(me + n - k, n)
            send(k, along, src, buf.at[frm], send_sem.at[k], recv_sem.at[k]).wait_recv()

    def group_lse(g, h, col, tile):
        lanes = slice(h * LANES, (h + 1) * LANES)
        tops, tots = [], []
        for i in range(GROUP):
            t = g * GROUP + i
            column = col(t, i)
            score = -tile[t, :, lanes] if column is None else column - tile[t, :, lanes]
            top = jnp.max(score, axis=0, keepdims=True)
            tops.append(top)
            tots.append(jnp.sum(jnp.exp2(score - top), axis=0, keepdims=True))
        at = pl.ds(pl.multiple_of(g * GROUP, GROUP), GROUP)
        slot_top[h, at, :] = jnp.concatenate(tops, axis=0)
        slot_tot[h, at, :] = jnp.concatenate(tots, axis=0)

    def slot_lse(h, ids):
        return jnp.where(ids >= 0, slot_top[h] + log2(slot_tot[h]), NEG)

    def as_column(row):
        return jnp.concatenate(
            [jnp.broadcast_to(row[:, h * LANES : (h + 1) * LANES], (LANES, LANES)).T for h in range(halves)], axis=0)

    eye = (lax.broadcasted_iota(jnp.int32, (bs, bs), 0) == lax.broadcasted_iota(jnp.int32, (bs, bs), 1))
    eye = eye.astype(jnp.float32).astype(jnp.bfloat16)
    for c in range(slots // GROUP):
        loads[c].wait()

        def turn(t, _):
            tile = tiles[t]
            turned = lax.dot_general(eye, tile, (((1,), (1,)), ((), ())), preferred_element_type=jnp.float32)
            tiles_t[t] = turned * LOG2E
            tiles_s[t] = tile.astype(jnp.float32) * LOG2E
            return 0

        lax.fori_loop(c * GROUP, (c + 1) * GROUP, turn, 0, unroll=2)
        for h in range(halves):
            group_lse(c, h, lambda t, i: None, tiles_t)

    pl.semaphore_wait(barrier, n_rows + n_cols - 2)
    cid_copies = exchange("rows", n_rows, my_r, cid, cid_all, cid_send, cid_recv)

    for t in range(slots):
        col_at = bcols[t] * halves
        for h in range(halves):
            lt_piece[h, t : t + 1, :] = log_tgt[pl.ds(col_at + h, 1), :] * LOG2E
    waits = list(cid_copies)
    block_of = lax.broadcasted_iota(jnp.int32, (row_blocks, LANES), 0)
    for sweep in range(ITERS):
        mine = []
        for h in range(halves):
            if sweep:
                def row_group(g, _):
                    at = pl.ds(pl.multiple_of(g * GROUP, GROUP), GROUP)
                    rows = jnp.concatenate([piece[k, at, :] for k in range(halves)], axis=1)

                    def column(t, i):
                        if h:
                            return columns[t]
                        made = as_column(rows[i : i + 1])
                        columns[t] = made
                        return made

                    group_lse(g, h, column, tiles_t)
                    return 0

                lax.fori_loop(0, slots // GROUP, row_group, 0)
            found = slot_lse(h, rid[...])
            masked = [jnp.where(block_of == rid[t : t + 1, :], found[t : t + 1, :], NEG) for t in range(slots)]
            top = functools.reduce(jnp.maximum, masked)
            total = functools.reduce(jnp.add, [jnp.exp2(value - top) for value in masked])
            part_src[h] = top + log2(total)
            mine += exchange("cols", n_cols, my_c, part_src.at[h], src_buf.at[sweep, h], src_send.at[sweep, h], src_recv.at[sweep, h])
            src_buf[sweep, h, pl.ds(my_c, 1)] = part_src[h][None]
        sources = []
        for h in range(halves):
            arrived("cols", n_cols, my_c, part_src.at[h], src_buf.at[sweep, h], src_send.at[sweep, h], src_recv.at[sweep, h])
            theirs = [src_buf[sweep, h, k] for k in range(n_cols)]
            top = functools.reduce(jnp.maximum, theirs)
            total = functools.reduce(jnp.add, [jnp.exp2(value - top) for value in theirs])
            source = log_src[pl.ds(h, row_blocks, stride=halves), :] * LOG2E - (top + log2(total))
            sources.append(source)
            for b in range(row_blocks):
                src_col[b, h * LANES : (h + 1) * LANES, :] = jnp.broadcast_to(source[b : b + 1, :], (LANES, LANES)).T
        for copy in mine:
            copy.wait_send()
        if sweep == 0:
            arrived("rows", n_rows, my_r, cid, cid_all, cid_send, cid_recv)
        mine = []
        for h in range(halves):
            def col_group(g, _):
                group_lse(g, h, lambda t, i: src_col[brows[t]], tiles_s)
                return 0

            lax.fori_loop(0, slots // GROUP, col_group, 0)
            part_tgt[h] = slot_lse(h, cid[...])
            mine += exchange("rows", n_rows, my_r, part_tgt.at[h], tgt_buf.at[sweep, h], tgt_send.at[sweep, h], tgt_recv.at[sweep, h])
            tgt_buf[sweep, h, pl.ds(my_r, 1)] = part_tgt[h][None]
        for h in range(halves):
            arrived("rows", n_rows, my_r, part_tgt.at[h], tgt_buf.at[sweep, h], tgt_send.at[sweep, h], tgt_recv.at[sweep, h])
            lanes = slice(h * LANES, (h + 1) * LANES)
            if sweep == ITERS - 1:
                for r in range(n_rows):
                    lse_out[r * slots : (r + 1) * slots, lanes] = tgt_buf[sweep, h, r]
                    ids_out[r * slots : (r + 1) * slots, :] = cid_all[r]
                src_out[:, lanes] = sources[h] * LN2
                continue
            ids = cid[...]

            def each(g):
                at = pl.ds(pl.multiple_of(g * GROUP, GROUP), GROUP)
                for r in range(n_rows):
                    theirs, values = cid_all[r, at, :], tgt_buf[sweep, h, r, at, :]
                    for i in range(GROUP):
                        yield jnp.where(ids == theirs[i : i + 1], values[i : i + 1], NEG)

            def top_of(g, top):
                return functools.reduce(jnp.maximum, each(g), top)

            top = lax.fori_loop(0, slots // GROUP, top_of, jnp.full(ids.shape, NEG, jnp.float32))

            def total_of(g, total):
                return functools.reduce(lambda so_far, value: so_far + jnp.exp2(value - top), each(g), total)

            total = lax.fori_loop(0, slots // GROUP, total_of, jnp.zeros(ids.shape, jnp.float32))
            piece[h] = jnp.where(ids >= 0, lt_piece[h] - (top + log2(total)), 0.0)
        for copy in mine:
            copy.wait_send()
    for copy in waits:
        copy.wait_send()


def final_kernel(source, lse, ids, log_tgt, src_out, tgt_out, top_buf):
    found, bs = lse.shape
    halves = bs // LANES
    blocks = tgt_out.shape[0] // halves
    exact = functools.partial(jnp.dot, preferred_element_type=jnp.float32, precision=lax.Precision.HIGHEST)
    per = 16 if blocks % 16 == 0 else blocks
    for b in range(0, blocks, per):
        block = lax.broadcasted_iota(jnp.int32, (per, LANES), 0) + b

        def top_of(g, top):
            at = pl.ds(pl.multiple_of(g * GROUP, GROUP), GROUP)
            theirs, values = ids[at, :], lse[at, :]
            for i in range(GROUP):
                here = jnp.concatenate([block == theirs[i : i + 1]] * halves, axis=1)
                top = jnp.maximum(top, jnp.where(here, values[i : i + 1], NEG))
            return top

        top_buf[b : b + per, :] = lax.fori_loop(
            0, found // GROUP, top_of, jnp.full((per, bs), NEG, jnp.float32), unroll=3 if found % (3 * GROUP) == 0 else 2)
    top = top_buf[...]
    names = ids[...].astype(jnp.float32)
    back = (names[:, 0:1] == lax.broadcasted_iota(jnp.int32, (found, blocks), 1).astype(jnp.float32)).astype(jnp.float32)
    into = (names.T[0:1, :] == lax.broadcasted_iota(jnp.int32, (blocks, found), 0).astype(jnp.float32)).astype(jnp.float32)
    total = exact(into, jnp.exp2(lse[...] - exact(back, top)))
    found_lse = top * LN2 + jnp.log(total)
    for h in range(halves):
        rows = pl.ds(h, blocks, stride=halves)
        tgt_out[rows, :] = log_tgt[rows, :] - found_lse[:, h * LANES : (h + 1) * LANES]
        src_out[pl.ds(h, source.shape[0], stride=halves), :] = source[:, h * LANES : (h + 1) * LANES]


def per_device(n_rows, n_cols, costs, block_rows, block_cols, live, log_source, log_target):
    tiles = costs[0, 0]
    slots, bs, _ = tiles.shape
    src_rows = log_source.shape[0] // LANES
    tgt_rows = log_target.shape[0] // LANES
    row_blocks = log_source.shape[0] // bs
    f32 = jnp.float32
    halves = bs // LANES
    dma = pltpu.SemaphoreType.DMA
    smem = pl.BlockSpec(memory_space=pltpu.SMEM)
    vmem = pl.BlockSpec(memory_space=pltpu.VMEM)
    found = n_rows * slots
    source, lse, ids = pl.pallas_call(
        functools.partial(kernel, n_rows, n_cols),
        out_shape=(
            jax.ShapeDtypeStruct((row_blocks, bs), f32),
            jax.ShapeDtypeStruct((found, bs), f32),
            jax.ShapeDtypeStruct((found, LANES), jnp.int32),
        ),
        in_specs=[smem, smem, smem, pl.BlockSpec(memory_space=pl.ANY), vmem, vmem],
        out_specs=(vmem, vmem, vmem),
        scratch_shapes=[
            pltpu.VMEM((slots, bs, bs), tiles.dtype),
            pltpu.VMEM((slots, bs, bs), f32),
            pltpu.VMEM((slots, bs, bs), f32),
            pltpu.VMEM((slots, LANES), jnp.int32),
            pltpu.VMEM((slots, LANES), jnp.int32),
            pltpu.VMEM((halves, slots, LANES), f32),
            pltpu.VMEM((halves, slots, LANES), f32),
            pltpu.VMEM((halves, row_blocks, LANES), f32),
            pltpu.VMEM((halves, slots, LANES), f32),
            pltpu.VMEM((slots, bs, LANES), f32),
            pltpu.VMEM((row_blocks, bs, LANES), f32),
            pltpu.VMEM((halves, slots, LANES), f32),
            pltpu.VMEM((halves, slots, LANES), f32),
            pltpu.VMEM((n_rows, slots, LANES), jnp.int32),
            pltpu.VMEM((ITERS, halves, n_cols, row_blocks, LANES), f32),
            pltpu.VMEM((ITERS, halves, n_rows, slots, LANES), f32),
            dma((slots // GROUP,)),
            dma((n_rows,)), dma((n_rows,)),
            dma((ITERS, halves, n_cols)), dma((ITERS, halves, n_cols)),
            dma((ITERS, halves, n_rows)), dma((ITERS, halves, n_rows)),
        ],
        compiler_params=pltpu.CompilerParams(collective_id=0, has_side_effects=True),
    )(
        block_rows.reshape(-1), block_cols.reshape(-1), live.reshape(-1), tiles,
        log_source.reshape(src_rows, LANES), log_target.reshape(tgt_rows, LANES),
    )
    source, target = pl.pallas_call(
        final_kernel,
        out_shape=(jax.ShapeDtypeStruct((src_rows, LANES), f32), jax.ShapeDtypeStruct((tgt_rows, LANES), f32)),
        in_specs=[vmem] * 4,
        out_specs=(vmem, vmem),
        scratch_shapes=[pltpu.VMEM((tgt_rows * LANES // bs, bs), f32)],
    )(source, lse, ids, log_target.reshape(tgt_rows, LANES))
    return source.reshape(-1), target.reshape(-1)


def solution(mesh):
    in_specs = (
        P("rows", "cols", None, None, None),
        P("rows", "cols", None),
        P("rows", "cols", None),
        P("rows", "cols"),
        P("rows"),
        P("cols"),
    )
    out_specs = (P("rows"), P("cols"))
    body = functools.partial(per_device, mesh.shape["rows"], mesh.shape["cols"])
    return jax.shard_map(body, mesh=mesh, in_specs=in_specs, out_specs=out_specs, check_vma=False)
```

time: 49.5 us -> 49.2 us (level)
  local copies, waits for them, and re-layouts: 2.38 us -> 0 us
  Pallas kernels: 45.4 us -> 47.7 us
    unnamed x8 -> x0, local copies, waits for them, and re-layouts: 2.38 us -> none
    pallas_call x1, Pallas kernels: 43.7 us -> 45 us  [per_device(): pl.pallas_call(functools.partial(kernel, n_rows, n_cols), out_shape=(jax....]
    pallas_call x1, Pallas kernels: 1.74 us -> 2.68 us  [per_device(): pl.pallas_call(final_kernel, out_shape=(jax.ShapeDtypeStruct((src_rows, L...]
where the time goes in v3:
time: 49.2 us; the launch traced here: 49 us
  Pallas kernels  47.7 us (97%)
  between operations  1.28 us (3%)
    pallas_call x1, Pallas kernels, per_device(): pl.pallas_call(functools.partial(kernel, n_rows, n_cols), out_shape=(jax....  45 us
    pallas_call x1, Pallas kernels, per_device(): pl.pallas_call(final_kernel, out_shape=(jax.ShapeDtypeStruct((src_rows, L...  2.68 us

profile of v3, /device:TPU:0, one launch (start us, length us, event | category | flops | bytes accessed | tf_op | source)
XLA Modules:
  0.0 49.0 jit_solution(4220222941400859727)
XLA Ops:
  1.3 45.0 %shard_map.77 = (f32[8,256]{1,0:T(8,128)}, f32[96,256]{1,0:T(8,128)}, s32[96,128]{1,0:T(8,128)}) custom-call(s32[24]{0:T(128)} %bitcast.13, s32[24]{0:T(128)} %bitcast.14, s32[1]{0:T(128)} %bitcast.8.live, bf16[24,256,256]{2,1,0:T(8,128)(2,1)} %bitcast.9, f32[16,128]{1,0:T(8,128)} %bitcast.12, f32[128,128]{1,0:T(8,128)} %bitcast.10), custom_call_target="tpu_custom_call" | custom-call | tf_op jit(solution)/shard_map/pallas_call | solution.py:250
  46.3 2.7 %shard_map.78 = (f32[16,128]{1,0:T(8,128)}, f32[128,128]{1,0:T(8,128)}) custom-call(f32[8,256]{1,0:T(8,128)} %get-tuple-element.7.source, f32[96,256]{1,0:T(8,128)} %get-tuple-element.8.lse, s32[96,128]{1,0:T(8,128)} %get-tuple-element.9.ids, f32[128,128]{1,0:T(8,128)} %bitcast.11), custom_call_target="tpu_custom_call" | custom-call | tf_op jit(solution)/shard_map/pallas_call | solution.py:286
